TPU v7x, 32 devices: a whole 2x2x4 slice. The times are simulated.
32 devices in a mesh: boot: 4 (over z), tm: 8 (over y, x, core).
Axes of the slice: x: 2, y: 2, z: 4, core: 2. Of those that a mesh axis runs over, the one named last changes fastest.
Arguments:
- recording: bfloat16 [4096, 1024], P('tm'), may hold values from -60 to 60, as said below
- starts: int32 [4, 48], P('boot', 'tm'), may hold values from 0 to 448, as said below
- lengths: int32 [4, 48], P('boot', 'tm'), may hold values from 1 to 64, as said below
- support: int32 [4, 4096], P(None, 'boot'), may hold values 0 or 1
Outputs:
- averaged: float32 [32, 4096], P(None, 'boot')
- residual: float32 [32, 4096], P(None, 'tm')
Inputs may be any that keep to these rules, and one draw needn't show every extreme that they name: A shard's values are an autoregressive recording; its values stay within the range. Entry [b, j * 6 + k] starts block k of resample b on time shard j, counted from the shard's first sample; a block ends inside its shard. The 6 lengths of one resample on one time shard sum to at most 384.
All inputs are finite; a program needn't handle non-finite values. No bound on the sum of `support` on one device may be relied on, other than what follows from the above.
Results may differ from a plain program's by a relative error of at most 0.0043.
The roundings to bfloat16 on the way count: a program that leaves them out, or rounds other values in their place, can miss the bound.
Values may be sent and summed in bfloat16 or wider, within the bound.
No kernel may reach another device: no remote copies, remote signals or barrier semaphores. Data moves between devices by JAX's collectives and lax.ppermute only.
A program may use at most 64 MiB of HBM per device.

v0:
```python
import jax
import jax.numpy as jnp
from jax import lax
from jax.sharding import PartitionSpec as P

CHANNEL_COUNT = 1024
LAGS = 4
RESPONSE_COUNT = 32
NBLK = 6
CAP = 384
ITERS = 3
CHEB = 5
ridge_weight = 4.0
shrink_level = 0.75
epsilon = 1e-05


def passed_along(block, axis, distance):
    devices = range(lax.axis_size(axis))
    route = [(i - distance, i) for i in devices if i - distance in devices]
    return lax.ppermute(block, axis, route)


def bootstrap_rows(window, begins, sizes):
    ends = jnp.cumsum(sizes)
    offsets = ends - sizes
    total = ends[-1]
    rows = jnp.arange(CAP, dtype=jnp.int32)
    member = (rows[:, None] >= offsets[None, :]).astype(jnp.int32)
    which = jnp.sum(member, axis=1) - 1
    picked = (which[:, None] == jnp.arange(NBLK, dtype=jnp.int32)[None, :]).astype(jnp.int32)
    anchor = jnp.sum(picked * offsets[None, :], axis=1)
    opening = jnp.sum(picked * begins[None, :], axis=1)
    live = rows < total
    times = jnp.where(live, opening + rows - anchor, 0)
    blocks = [jnp.take(window, times + LAGS - 1 - delay_step, axis=0) for delay_step in range(LAGS)]
    design = jnp.concatenate(blocks, axis=1)
    design = jnp.where(live[:, None], design, jnp.zeros_like(design))
    answer = jnp.take(window[:, :RESPONSE_COUNT], times + LAGS, axis=0)
    answer = jnp.where(live[:, None], answer, jnp.zeros_like(answer))
    return (design, answer.T)


def chebyshev(gram, rhs, bound):
    center = ridge_weight + 0.5 * bound
    radius = 0.5 * bound
    sigma = center / radius
    solution = jnp.zeros_like(rhs)
    remain = rhs
    factor = 1.0 / sigma
    update = rhs / center
    for count in range(CHEB):
        solution = solution + update
        if count + 1 < CHEB:
            applied = ridge_weight * update + jnp.einsum(
                "brc,bcd->brd", update, gram, precision=lax.Precision.HIGHEST
            )
            remain = remain - applied
            after = 1.0 / (2.0 * sigma - factor)
            update = after * factor * update + 2.0 * after / radius * remain
            factor = after
    return solution


def shrink_columns(mean_value, norms, level):
    return mean_value * (jnp.maximum(norms - level, 0.0) / jnp.maximum(norms, level))[:, None, :]


def per_device(recording, starts, lengths, support):
    shards = lax.axis_size("tm")
    samples = recording.shape[0]
    values = recording.astype(jnp.float32)
    power = lax.psum(jnp.sum(values * values, axis=0), "tm")
    scale = 1.0 / jnp.sqrt(power / (samples * shards) + epsilon)
    scaled_input = (values * scale).astype(jnp.bfloat16)
    carried = passed_along(scaled_input[samples - LAGS :], "tm", 1)
    extended = jnp.concatenate([carried, scaled_input], axis=0)
    design, answer = jax.vmap(bootstrap_rows, in_axes=(None, 0, 0))(extended, starts, lengths)
    row_scale = 1.0 / CAP
    cross = (
        jnp.einsum("brc,bcf->brf", answer, design, preferred_element_type=jnp.float32) * row_scale
    )
    gram = (
        jnp.einsum("bcf,bdf->bcd", design, design, preferred_element_type=jnp.float32) * row_scale
    )
    bound = jnp.sqrt(jnp.sum(gram * gram, axis=(1, 2)))[:, None, None]
    consensus = jnp.zeros_like(cross)
    dual = jnp.zeros_like(cross)
    for rounds in range(ITERS):
        target = cross + ridge_weight * (consensus - dual)
        projected = (
            jnp.einsum(
                "brf,bcf->brc",
                target.astype(jnp.bfloat16),
                design,
                preferred_element_type=jnp.float32,
            )
            * row_scale
        )
        weights = chebyshev(gram, projected, bound)
        back = jnp.einsum(
            "brc,bcf->brf", weights.astype(jnp.bfloat16), design, preferred_element_type=jnp.float32
        )
        local = (target - back) / ridge_weight
        stacked = local + dual
        mean_value = lax.psum(stacked, "tm") / shards
        norms = jnp.sqrt(jnp.sum(mean_value * mean_value, axis=1))
        level = shrink_level * jnp.mean(norms, axis=1, keepdims=True)
        consensus = shrink_columns(mean_value, norms, level)
        dual = dual + local - consensus
    width = consensus.shape[2] // lax.axis_size("boot")
    position = lax.axis_index("boot")
    chosen = support.astype(jnp.float32)
    tally = jnp.sum(chosen, axis=0)
    mine = lax.all_to_all(support, "boot", split_axis=0, concat_axis=1, tiled=True).astype(
        jnp.float32
    )
    weighted = jnp.sum(mine[:, None, :] * consensus, axis=0)
    summed = lax.psum_scatter(weighted, "boot", scatter_dimension=1, tiled=True)
    averaged = summed / jnp.maximum(tally, 1.0)[None, :]
    opening = position * width
    delay_step = opening // CHANNEL_COUNT
    channel = opening % CHANNEL_COUNT
    columns = lax.dynamic_slice(extended, (LAGS - 1 - delay_step, channel), (samples, width))
    partial_result = lax.dot_general(
        averaged.astype(jnp.bfloat16),
        columns,
        (((1,), (1,)), ((), ())),
        preferred_element_type=jnp.float32,
    )
    predicted_output = lax.psum(partial_result, "boot")
    residual = scaled_input[:, :RESPONSE_COUNT].astype(jnp.float32).T - predicted_output
    return (averaged, residual)


def solution(mesh):
    in_specs = (P("tm", None), P("boot", "tm"), P("boot", "tm"), P(None, "boot"))
    out_specs = (P(None, "boot"), P(None, "tm"))
    return jax.shard_map(
        per_device, mesh=mesh, in_specs=in_specs, out_specs=out_specs, check_vma=False
    )
```

profile of v0, /device:TPU:0, one launch (start us, length us, event | category | flops | bytes accessed | tf_op | source)
XLA Modules:
  0.0 315.7 jit_solution(589085711330140276)
XLA Ops:
  7.2 1.5 copy.24
  9.0 15.2 %psum.35 = f32[1024]{0:T(1024)S(1)} all-reduce(f32[1024]{0:T(1024)S(1)} %fusion.9), channel_id=1, replica_groups=mesh['boot'=4,'tm'=8] {'tm'}, use_global_device_ids=true, to_apply=%region_5.6 | all-reduce | flops 1024 | bytes 8192 | tf_op jit(solution)/shard_map/psum | solution.py:73
  31.1 2.7 gather_fusion.4
  33.8 2.7 gather_fusion.3
  36.5 2.7 gather_fusion.2
  39.2 2.7 gather_fusion.1
  41.9 2.7 fusion.38
  46.8 2.5 multiply_reduce_fusion
  50.7 1.4 gather_fusion
  52.1 2.7 convolution_multiply_fusion
  54.8 2.1 maximum_select_fusion.1
  59.7 1.5 fusion.1
  61.5 58.2 %all-reduce.5.cloned.1.call-done = f32[1,32,4096]{2,1,0:T(8,128)} async-done(((f32[1,32,4096]{2,1,0:T(8,128)}), f32[1,32,4096]{2,1,0:T(8,128)}) %all-reduce.5.cloned.1.call-update) | async-done | bytes 524304 | tf_op jit(solution)/shard_map/psum | solution.py:106
  122.1 3.4 %convolution_multiply_fusion.3 = f32[32,384]{1,0:T(8,128)S(1)} fusion(bf16[384,4096]{1,0:T(8,128)(2,1)} %copy-done.3, f32[1,32,4096]{2,1,0:T(8,128)} %fusion.1, f32[1,32,4096]{2,1,0:T(8,128)} %all-reduce.5.cloned.1.call-done, f32[32,4096]{1,0:T(8,128)S(1)} %convolution_multiply_fusion, f32[4096]{0:T(1024)S(1)} %divide_multiply_fusion.2), kind=kOutput, calls=%fused_computation.31 | convolution fusion | flops 101462016 | bytes 4784128 | tf_op jit(solution)/shard_map/brf,bcf->brc/dot_general | solution.py:92
  127.3 1.5 fusion.7
  129.0 54.2 %all-reduce.7.cloned.1.call-done = f32[1,32,4096]{2,1,0:T(8,128)} async-done(((f32[1,32,4096]{2,1,0:T(8,128)}), f32[1,32,4096]{2,1,0:T(8,128)}) %all-reduce.7.cloned.1.call-update) | async-done | bytes 524304 | tf_op jit(solution)/shard_map/psum | solution.py:106
  185.6 3.4 %convolution_multiply_fusion.2 = f32[32,384]{1,0:T(8,128)S(1)} fusion(bf16[384,4096]{1,0:T(8,128)(2,1)} %copy-done.3, f32[1,32,4096]{2,1,0:T(8,128)} %fusion.7, f32[1,32,4096]{2,1,0:T(8,128)} %all-reduce.7.cloned.1.call-done, f32[32,4096]{1,0:T(8,128)S(1)} %convolution_multiply_fusion, f32[4096]{0:T(1024)S(1)} %divide_multiply_fusion.1), kind=kOutput, calls=%fused_computation.30 | convolution fusion | flops 101462016 | bytes 4784128 | tf_op jit(solution)/shard_map/brf,bcf->brc/dot_general | solution.py:92
  190.9 1.5 fusion.4
  192.5 9.9 %all_to_all.13 = s32[4,1,1024]{2,1,0:T(1,128)S(1)} all-to-all(s32[4,1,1024]{2,1,0:T(1,128)S(1)} %all_to_all.10), channel_id=1, replica_groups=mesh['boot'=4,'tm'=8] {'boot'}, dimensions={0} | all-to-all | bytes 32768 | tf_op jit(solution)/shard_map/all_to_all | solution.py:115
  202.5 44.2 %all-reduce.9.cloned.1.call-done = f32[1,32,4096]{2,1,0:T(8,128)} async-done(((f32[1,32,4096]{2,1,0:T(8,128)}), f32[1,32,4096]{2,1,0:T(8,128)}) %all-reduce.9.cloned.1.call-update) | async-done | bytes 524304 | tf_op jit(solution)/shard_map/psum | solution.py:106
  249.1 1.9 multiply_bitcast_fusion
  251.1 21.2 %reduce-scatter.2.cloned.1.call-done = f32[32,1024]{1,0:T(8,128)} async-done(((f32[32,4096]{1,0:T(8,128)}), f32[32,1024]{1,0:T(8,128)}) %reduce-scatter.2.cloned.1.call-update) | async-done | bytes 131088 | tf_op jit(solution)/shard_map/reduce_scatter | solution.py:119
  274.6 33.1 %all-reduce.11.cloned.1.call-done = f32[32,512]{1,0:T(8,128)} async-done(((f32[32,512]{1,0:T(8,128)}), f32[32,512]{1,0:T(8,128)}) %all-reduce.11.cloned.1.call-update) | async-done | bytes 65552 | tf_op jit(solution)/shard_map/psum | solution.py:131
  307.7 1.5 bitcast_subtract_fusion
  (97 shorter events, 24.0 us)
Async XLA Ops:
  7.2 18.8 %copy-start.15 = (s32[1,6]{1,0:T(1,128)S(1)}, s32[1,6]{1,0:T(1,128)}, u32[]{:S(2)}) copy-start(s32[1,6]{1,0:T(1,128)} %param.8) | copy-start | bytes 76
  7.2 19.6 %copy-start.14 = (s32[1,6]{1,0:T(1,128)S(1)}, s32[1,6]{1,0:T(1,128)}, u32[]{:S(2)}) copy-start(s32[1,6]{1,0:T(1,128)} %param.7) | copy-start | bytes 76
  7.2 112.5 %all-reduce.5.cloned.1.call-start = ((), (), s32[]{:S(2)}) async-start(), calls=%async_computation.2 | async-start | bytes 1048576 | tf_op jit(solution)/shard_map/psum | solution.py:106
  24.6 4.4 %collective-permute-start = (bf16[4,1024]{0,1:T(8,128)(2,1)S(1)}, bf16[4,1024]{0,1:T(8,128)(2,1)S(1)}, u32[]{:S(2)}, u32[]{:S(2)}) collective-permute-start(bf16[4,1024]{0,1:T(8,128)(2,1)S(1)} %slice.26), channel_id=1, source_target_pairs={{0,1},{1,2},{2,3},{3,4},{4,5},{5,6},{6,7},{8,9},{9,10},{10,11},{11... | collective-permute-start | bytes 24584 | tf_op jit(solution)/shard_map/ppermute | solution.py:21
  29.1 0.7 copy-start.10
  41.9 2.7 copy-start.8
  41.9 2.7 copy-start.9
  46.8 2.5 copy-start.3
  46.8 3.4 %copy-start.11 = (bf16[4,1024]{0,1:T(8,128)(2,1)S(1)}, bf16[4,1024]{0,1:T(8,128)(2,1)}, u32[]{:S(2)}) copy-start(bf16[4,1024]{0,1:T(8,128)(2,1)} %copy-done.10) | copy-start | bytes 24580
  56.9 2.8 copy-start
  61.3 121.9 %all-reduce.7.cloned.1.call-start = ((), (), s32[]{:S(2)}) async-start(), calls=%async_computation.3 | async-start | bytes 1048576 | tf_op jit(solution)/shard_map/psum | solution.py:106
  122.1 5.2 %copy-start.1 = (bf16[384,4096]{1,0:T(8,128)(2,1)S(1)}, bf16[384,4096]{1,0:T(8,128)(2,1)}, u32[]{:S(2)}) copy-start(bf16[384,4096]{1,0:T(8,128)(2,1)} %copy-done) | copy-start | bytes 9437188
  122.1 5.2 %copy-start.5 = (f32[1,32,4096]{2,1,0:T(8,128)S(1)}, f32[1,32,4096]{2,1,0:T(8,128)}, u32[]{:S(2)}) copy-start(f32[1,32,4096]{2,1,0:T(8,128)} %fusion.1) | copy-start | bytes 1572868
  122.1 5.2 %copy-start.7 = (f32[1,32,4096]{2,1,0:T(8,128)S(1)}, f32[1,32,4096]{2,1,0:T(8,128)}, u32[]{:S(2)}) copy-start(f32[1,32,4096]{2,1,0:T(8,128)} %all-reduce.5.cloned.1.call-done) | copy-start | bytes 1572868
  128.9 117.8 %all-reduce.9.cloned.1.call-start = ((), (), s32[]{:S(2)}) async-start(), calls=%async_computation.4 | async-start | bytes 1048576 | tf_op jit(solution)/shard_map/psum | solution.py:106
  185.6 5.2 %copy-start.2 = (bf16[384,4096]{1,0:T(8,128)(2,1)S(1)}, bf16[384,4096]{1,0:T(8,128)(2,1)}, u32[]{:S(2)}) copy-start(bf16[384,4096]{1,0:T(8,128)(2,1)} %copy-done) | copy-start | bytes 9437188
  185.6 5.2 %copy-start.4 = (f32[1,32,4096]{2,1,0:T(8,128)S(1)}, f32[1,32,4096]{2,1,0:T(8,128)}, u32[]{:S(2)}) copy-start(f32[1,32,4096]{2,1,0:T(8,128)} %fusion.7) | copy-start | bytes 1572868
  185.6 5.2 %copy-start.6 = (f32[1,32,4096]{2,1,0:T(8,128)S(1)}, f32[1,32,4096]{2,1,0:T(8,128)}, u32[]{:S(2)}) copy-start(f32[1,32,4096]{2,1,0:T(8,128)} %all-reduce.7.cloned.1.call-done) | copy-start | bytes 1572868
  190.4 2.1 copy-start.13
  192.4 79.9 %reduce-scatter.2.cloned.1.call-start = ((), (), s32[]{:S(2)}) async-start(), calls=%async_computation.5 | async-start | bytes 655360 | tf_op jit(solution)/shard_map/reduce_scatter | solution.py:119
  251.0 56.6 %all-reduce.11.cloned.1.call-start = ((), (), s32[]{:S(2)}) async-start(), calls=%async_computation.6 | async-start | bytes 131072 | tf_op jit(solution)/shard_map/psum | solution.py:131
  273.3 35.9 %copy-start.12 = (f32[32,1024]{1,0:T(8,128)}, f32[32,1024]{1,0:T(8,128)S(1)}, u32[]{:S(2)}) copy-start(f32[32,1024]{1,0:T(8,128)S(1)} %broadcast_divide_fusion) | copy-start | bytes 393220
Sparse Core Ops, SparseCore 0:
  61.4 58.2 all-reduce.4
  129.0 54.1 all-reduce.6
  192.5 54.1 all-reduce.8
  251.2 21.1 reduce-scatter.1
  275.1 32.5 all-reduce.10
where the time goes:
time: 316 us
  waiting for transfers between devices  211 us (67%)
  blocking collectives  25.1 us (8%)
  matrix products  24 us (8%)
  other arithmetic  20.6 us (7%)
  between operations  17.4 us (6%)
  local copies, waits for them, and re-layouts  15.9 us (5%)
    psum x3, waiting for transfers between devices, per_device(): mean_value = lax.psum(stacked, 'tm') / shards  157 us
    psum x1, waiting for transfers between devices, per_device(): predicted_output = lax.psum(partial_result, 'boot')  33.1 us
    reduce_scatter x1, waiting for transfers between devices, per_device(): summed = lax.psum_scatter(weighted, 'boot', scatter_dimension=1, tiled=True)  21.2 us
    psum x1, blocking collectives, per_device(): power = lax.psum(jnp.sum(values * values, axis=0), 'tm')  15.2 us
    gather x4, local copies, waits for them, and re-layouts, bootstrap_rows(): jnp.take(window, times + LAGS - 1 - delay_step, axis=0)  10.8 us
    all_to_all x1, blocking collectives, per_device(): lax.all_to_all(support, 'boot', split_axis=0, concat_axis=1, tiled=True)  9.94 us
    dot_general x3, matrix products, per_device(): jnp.einsum('brf,bcf->brc', target.astype(jnp.bfloat16), design, preferred...  7.84 us
  transfers between devices with their start and end apart: 6, of which 5 were waited for; matrix products, arithmetic and copies ran while one was open for 1% of the time, Pallas kernels for 0%

commit v1 on v0

--- a/solution.py
+++ b/solution.py
@@ -2,6 +2,7 @@
 import jax.numpy as jnp
 from jax import lax
 from jax.sharding import PartitionSpec as P
+from jax.lax import all_gather
 
 CHANNEL_COUNT = 1024
 LAGS = 4
@@ -13,6 +14,10 @@
 ridge_weight = 4.0
 shrink_level = 0.75
 epsilon = 1e-05
+
+
+def perform_pages(t0):
+    return jnp.sum(all_gather(t0, "tm"), axis=0)
 
 
 def passed_along(block, axis, distance):
@@ -103,7 +108,7 @@
         )
         local = (target - back) / ridge_weight
         stacked = local + dual
-        mean_value = lax.psum(stacked, "tm") / shards
+        mean_value = perform_pages(stacked) / shards
         norms = jnp.sqrt(jnp.sum(mean_value * mean_value, axis=1))
         level = shrink_level * jnp.mean(norms, axis=1, keepdims=True)
         consensus = shrink_columns(mean_value, norms, level)

time: 316 us -> 269 us (0.85)
  waiting for transfers between devices: 211 us -> 158 us
  other arithmetic: 20.6 us -> 27.7 us
    psum x3 -> x0, waiting for transfers between devices: 157 us -> none  [per_device(): mean_value = lax.psum(stacked, 'tm') / shards]
    all_gather x0 -> x3, waiting for transfers between devices: none -> 103 us  [perform_pages(): return jnp.sum(all_gather(t0, 'tm'), axis=0)]
    reduce_sum x1 -> x3, other arithmetic: 1.9 us -> 9.03 us  [perform_pages(): return jnp.sum(all_gather(t0, 'tm'), axis=0)]
where the time goes in v1:
time: 269 us; the launch traced here: 268 us
  waiting for transfers between devices  158 us (59%)
  other arithmetic  27.7 us (10%)
  blocking collectives  25.2 us (9%)
  matrix products  22.3 us (8%)
  between operations  17.5 us (7%)
  local copies, waits for them, and re-layouts  15.3 us (6%)
    all_gather x3, waiting for transfers between devices, perform_pages(): return jnp.sum(all_gather(t0, 'tm'), axis=0)  103 us
    psum x1, waiting for transfers between devices, per_device(): predicted_output = lax.psum(partial_result, 'boot')  33.1 us
    reduce_scatter x1, waiting for transfers between devices, per_device(): summed = lax.psum_scatter(weighted, 'boot', scatter_dimension=1, tiled=True)  21.9 us
    psum x1, blocking collectives, per_device(): power = lax.psum(jnp.sum(values * values, axis=0), 'tm')  15.2 us
    all_to_all x1, blocking collectives, per_device(): lax.all_to_all(support, 'boot', split_axis=0, concat_axis=1, tiled=True)  10 us
    gather x4, local copies, waits for them, and re-layouts, bootstrap_rows(): jnp.take(window, times + LAGS - 1 - delay_step, axis=0)  9.54 us
    reduce_sum x3, other arithmetic, perform_pages(): return jnp.sum(all_gather(t0, 'tm'), axis=0)  9.03 us
    dot_general x3, matrix products, per_device(): jnp.einsum('brf,bcf->brc', target.astype(jnp.bfloat16), design, preferred...  6.13 us
  transfers between devices with their start and end apart: 6, of which 5 were waited for; matrix products, arithmetic and copies ran while one was open for 1% of the time, Pallas kernels for 0%

profile of v1, /device:TPU:0, one launch (start us, length us, event | category | flops | bytes accessed | tf_op | source)
XLA Modules:
  0.0 267.9 jit_solution(12484436035894477531)
XLA Ops:
  7.2 1.5 copy.24
  9.0 15.2 %psum.14 = f32[1024]{0:T(1024)S(1)} all-reduce(f32[1024]{0:T(1024)S(1)} %fusion.6), channel_id=1, replica_groups=mesh['boot'=4,'tm'=8] {'tm'}, use_global_device_ids=true, to_apply=%region_5.6 | all-reduce | flops 1024 | bytes 8192 | tf_op jit(solution)/shard_map/psum | solution.py:78
  30.4 2.7 %gather_fusion.1 = bf16[384,1024]{1,0:T(8,128)(2,1)} fusion(bf16[516,1024]{1,0:T(8,128)(2,1)S(1)} %copy.26, s32[1024]{0:T(1024)S(1)} %pad_clamp_fusion.3), kind=kCustom, calls=%fused_computation.clone | custom fusion | bytes 1574400 | tf_op jit(solution)/shard_map/vmap(jit(_take))/gather | solution.py:41
  33.1 2.7 %gather_fusion.2 = bf16[384,1024]{1,0:T(8,128)(2,1)} fusion(bf16[516,1024]{1,0:T(8,128)(2,1)S(1)} %copy.26, s32[1024]{0:T(1024)S(1)} %pad_clamp_fusion.2), kind=kCustom, calls=%fused_computation.1.clone | custom fusion | bytes 1574400 | tf_op jit(solution)/shard_map/vmap(jit(_take))/gather | solution.py:41
  35.8 2.1 gather_fusion.4
  37.9 2.1 gather_fusion.3
  40.0 2.8 %fusion.36 = (bf16[1,384,1,1,1,1,1024]{6,1,5,4,3,2,0:T(8,128)(2,1)S(1)}, bf16[384,1024]{1,0:T(8,128)(2,1)}, bf16[384,1024]{1,0:T(8,128)(2,1)}, bf16[1,384,1,1,1,1,1024]{6,1,5,4,3,2,0:T(8,128)(2,1)S(1)}) fusion(bf16[384,1024]{1,0:T(8,128)(2,1)} %gather_fusion.1, pred[384]{0:T(512)(128)(4,1)S(1)} %get-tuple-element.5, bf16[384,1024]{1,0:T(8,128)(2,1)} %gather_fusion.2, ...), kind=kLoop, calls=%fused_computation.80 | loop fusion | flops 786432 | bytes 4719360 | tf_op jit(solution)/shard_map/vmap()/concatenate | solution.py:42
  45.1 3.2 %multiply_reduce_fusion = (f32[]{:T(128)}, f32[384,384]{1,0:T(8,128)}) fusion(bf16[384,4096]{1,0:T(8,128)(2,1)S(1)} %fusion.5), kind=kOutput, calls=%fused_computation.72 | convolution fusion | flops 1208401920 | bytes 3735556 | tf_op jit(solution)/shard_map/bcf,bdf->bcd/dot_general | solution.py:89
  51.8 1.9 gather_fusion
  53.7 1.8 convolution_multiply_fusion
  59.3 1.5 fusion.2
  61.0 40.0 %all-gather.7.cloned.1.call-done = f32[256,4096]{1,0:T(8,128)} async-done(((f32[32,4096]{1,0:T(8,128)}), f32[256,4096]{1,0:T(8,128)}) %all-gather.7.cloned.1.call-update) | async-done | bytes 4194320 | tf_op jit(solution)/shard_map/all_gather | solution.py:20
  101.0 3.3 %reduce.20 = f32[32,4096]{1,0:T(8,128)} reduce(f32[8,32,4096]{2,1,0:T(8,128)} %bitcast.97, f32[]{:T(128)} %constant.108.clone.1), dimensions={0}, to_apply=%region_7.9 | reduce | flops 917504 | bytes 4718596 | tf_op jit(solution)/shard_map/reduce_sum | solution.py:20
  106.7 2.5 convolution_multiply_fusion.3
  111.1 1.5 fusion.3
  112.7 36.7 %all-gather.9.cloned.1.call-done = f32[256,4096]{1,0:T(8,128)} async-done(((f32[32,4096]{1,0:T(8,128)}), f32[256,4096]{1,0:T(8,128)}) %all-gather.9.cloned.1.call-update) | async-done | bytes 4194320 | tf_op jit(solution)/shard_map/all_gather | solution.py:20
  149.4 3.3 %reduce.21 = f32[32,4096]{1,0:T(8,128)} reduce(f32[8,32,4096]{2,1,0:T(8,128)} %bitcast.98, f32[]{:T(128)} %constant.108.clone.1), dimensions={0}, to_apply=%region_10.12 | reduce | flops 917504 | bytes 4718596 | tf_op jit(solution)/shard_map/reduce_sum | solution.py:20
  155.1 2.5 convolution_multiply_fusion.2
  159.5 1.5 fusion.4
  161.1 10.0 %all_to_all.13 = s32[4,1,1024]{2,1,0:T(1,128)S(1)} all-to-all(s32[4,1,1024]{2,1,0:T(1,128)S(1)} %all_to_all.10), channel_id=1, replica_groups=mesh['boot'=4,'tm'=8] {'boot'}, dimensions={0} | all-to-all | bytes 32768 | tf_op jit(solution)/shard_map/all_to_all | solution.py:120
  171.1 26.6 %all-gather.11.cloned.1.call-done = f32[256,4096]{1,0:T(8,128)} async-done(((f32[32,4096]{1,0:T(8,128)}), f32[256,4096]{1,0:T(8,128)}) %all-gather.11.cloned.1.call-update) | async-done | bytes 4194320 | tf_op jit(solution)/shard_map/all_gather | solution.py:20
  197.7 2.5 reduce.22
  202.6 21.9 %reduce-scatter.2.cloned.1.call-done = f32[32,1024]{1,0:T(8,128)} async-done(((f32[32,4096]{1,0:T(8,128)}), f32[32,1024]{1,0:T(8,128)}) %reduce-scatter.2.cloned.1.call-update) | async-done | bytes 131088 | tf_op jit(solution)/shard_map/reduce_scatter | solution.py:124
  226.7 33.1 %all-reduce.2.cloned.1.call-done = f32[32,512]{1,0:T(8,128)} async-done(((f32[32,512]{1,0:T(8,128)}), f32[32,512]{1,0:T(8,128)}) %all-reduce.2.cloned.1.call-update) | async-done | bytes 65552 | tf_op jit(solution)/shard_map/psum | solution.py:136
  (108 shorter events, 27.5 us)
Async XLA Ops:
  7.2 18.8 %copy-start.19 = (s32[1,6]{1,0:T(1,128)S(1)}, s32[1,6]{1,0:T(1,128)}, u32[]{:S(2)}) copy-start(s32[1,6]{1,0:T(1,128)} %param.8) | copy-start | bytes 76
  7.2 19.6 %copy-start.18 = (s32[1,6]{1,0:T(1,128)S(1)}, s32[1,6]{1,0:T(1,128)}, u32[]{:S(2)}) copy-start(s32[1,6]{1,0:T(1,128)} %param.7) | copy-start | bytes 76
  7.2 93.8 %all-gather.7.cloned.1.call-start = ((), (), s32[]{:S(2)}) async-start(), calls=%async_computation.4 | async-start | bytes 4718592 | tf_op jit(solution)/shard_map/all_gather | solution.py:20
  24.5 4.6 %copy-start.6 = (bf16[512,1024]{0,1:T(8,128)(2,1)}, bf16[512,1024]{0,1:T(8,128)(2,1)S(1)}, u32[]{:S(2)}) copy-start(bf16[512,1024]{0,1:T(8,128)(2,1)S(1)} %fusion.7) | copy-start | bytes 3145732
  24.6 4.4 %collective-permute-start = (bf16[4,1024]{0,1:T(8,128)(2,1)S(1)}, bf16[4,1024]{0,1:T(8,128)(2,1)S(1)}, u32[]{:S(2)}, u32[]{:S(2)}) collective-permute-start(bf16[4,1024]{0,1:T(8,128)(2,1)S(1)} %slice.26), channel_id=1, source_target_pairs={{0,1},{1,2},{2,3},{3,4},{4,5},{5,6},{6,7},{8,9},{9,10},{10,11},{11... | collective-permute-start | bytes 24584 | tf_op jit(solution)/shard_map/ppermute | solution.py:26
  53.7 1.8 copy-start.13
  53.7 1.9 copy-start.14
  53.7 1.9 copy-start.15
  55.5 3.8 %copy-start.3 = (f32[32,4096]{1,0:T(8,128)}, f32[32,4096]{1,0:T(8,128)S(1)}, u32[]{:S(2)}) copy-start(f32[32,4096]{1,0:T(8,128)S(1)} %convolution_multiply_fusion) | copy-start | bytes 1572868
  60.8 88.5 %all-gather.9.cloned.1.call-start = ((), (), s32[]{:S(2)}) async-start(), calls=%async_computation.5 | async-start | bytes 4718592 | tf_op jit(solution)/shard_map/all_gather | solution.py:20
  106.6 2.6 copy-start.1
  106.7 4.4 %copy-start.4 = (f32[32,4096]{1,0:T(8,128)S(1)}, f32[32,4096]{1,0:T(8,128)}, u32[]{:S(2)}) copy-start(f32[32,4096]{1,0:T(8,128)} %copy-done.3) | copy-start | bytes 1572868
  106.7 4.4 %copy-start.10 = (f32[32,4096]{1,0:T(8,128)S(1)}, f32[32,4096]{1,0:T(8,128)}, u32[]{:S(2)}) copy-start(f32[32,4096]{1,0:T(8,128)} %reduce.20) | copy-start | bytes 1572868
  106.7 4.4 %copy-start.11 = (f32[32,4096]{1,0:T(8,128)S(1)}, f32[32,4096]{1,0:T(8,128)}, u32[]{:S(2)}) copy-start(f32[32,4096]{1,0:T(8,128)} %fusion.2) | copy-start | bytes 1572868
  112.6 85.1 %all-gather.11.cloned.1.call-start = ((), (), s32[]{:S(2)}) async-start(), calls=%async_computation.6 | async-start | bytes 4718592 | tf_op jit(solution)/shard_map/all_gather | solution.py:20
  155.0 2.6 copy-start.2
  155.0 4.4 %copy-start.5 = (f32[32,4096]{1,0:T(8,128)S(1)}, f32[32,4096]{1,0:T(8,128)}, u32[]{:S(2)}) copy-start(f32[32,4096]{1,0:T(8,128)} %copy-done.3) | copy-start | bytes 1572868
  155.1 4.4 %copy-start.8 = (f32[32,4096]{1,0:T(8,128)S(1)}, f32[32,4096]{1,0:T(8,128)}, u32[]{:S(2)}) copy-start(f32[32,4096]{1,0:T(8,128)} %fusion.3) | copy-start | bytes 1572868
  155.1 4.4 %copy-start.9 = (f32[32,4096]{1,0:T(8,128)S(1)}, f32[32,4096]{1,0:T(8,128)}, u32[]{:S(2)}) copy-start(f32[32,4096]{1,0:T(8,128)} %reduce.21) | copy-start | bytes 1572868
  159.0 2.1 copy-start.17
  161.0 63.5 %reduce-scatter.2.cloned.1.call-start = ((), (), s32[]{:S(2)}) async-start(), calls=%async_computation.2 | async-start | bytes 655360 | tf_op jit(solution)/shard_map/reduce_scatter | solution.py:124
  197.7 27.7 %copy-start.7 = (bf16[512,1024]{0,1:T(8,128)(2,1)S(1)}, bf16[512,1024]{0,1:T(8,128)(2,1)}, u32[]{:S(2)}) copy-start(bf16[512,1024]{0,1:T(8,128)(2,1)} %copy-done.6) | copy-start | bytes 3145732
  202.5 57.3 %all-reduce.2.cloned.1.call-start = ((), (), s32[]{:S(2)}) async-start(), calls=%async_computation.3 | async-start | bytes 131072 | tf_op jit(solution)/shard_map/psum | solution.py:136
  225.4 35.9 %copy-start.16 = (f32[32,1024]{1,0:T(8,128)}, f32[32,1024]{1,0:T(8,128)S(1)}, u32[]{:S(2)}) copy-start(f32[32,1024]{1,0:T(8,128)S(1)} %broadcast_divide_fusion) | copy-start | bytes 393220
  (2 other events, 2.9 us)
Sparse Core Ops, SparseCore 0:
  60.9 40.0 all-gather.6
  112.8 36.5 all-gather.8
  161.1 36.5 all-gather.10
  202.6 21.8 reduce-scatter.1
  227.2 32.5 all-reduce.1
